TPU v7x, 128 devices: a whole 4x4x4 slice. The times are simulated.
128 devices in a mesh: shard: 8 (over y_lo, z), ctx: 4 (over x), tp: 4 (over y_hi, core).
Axes of the slice: x: 4, y: 4 (y_hi: 2, y_lo: 2; y = y_hi * 2 + y_lo), z: 4, core: 2. Of those that a mesh axis runs over, the one named last changes fastest.
Arguments:
- tokens: bfloat16 [16, 1376, 1024], P('shard', 'ctx'), may hold values from -6 to 6
- cotangent: bfloat16 [16, 1376, 1024], P('shard', 'ctx'), may hold values from -6 to 6
- slot_live: int32 [16], P('shard'), may hold values from 0 to 1, as said below
- block_rows: int32 [16, 4], P('shard'), may hold values from 1 to 344, 1370 in all within a row
- ln1_gain: float32 [1024], replicated, may hold values from 0.1 to 1.9
- ln1_bias: float32 [1024], replicated, may hold values from -3 to 3
- w_qkv: bfloat16 [1024, 3, 1024], P(('shard', 'ctx'), None, 'tp'), may hold values from -0.1875 to 0.1875
- b_qv: float32 [2, 1024], P(None, 'tp'), may hold values from -3 to 3
- w_proj: bfloat16 [1024, 1024], P(('shard', 'ctx'), 'tp'), may hold values from -1.5 to 1.5
- b_proj: float32 [1024], replicated, may hold values from -3 to 3
- scale_attn: float32 [1024], replicated, may hold values from 0.1 to 1.9
- ln2_gain: float32 [1024], replicated, may hold values from 0.1 to 1.9
- ln2_bias: float32 [1024], replicated, may hold values from -3 to 3
- w_up: bfloat16 [1024, 4096], P(('shard', 'ctx'), 'tp'), may hold values from -0.1875 to 0.1875
- b_up: float32 [4096], P('tp'), may hold values from -3 to 3
- w_down: bfloat16 [1024, 4096], P(('shard', 'ctx'), 'tp'), may hold values from -0.09375 to 0.09375
- b_down: float32 [1024], replicated, may hold values from -3 to 3
- scale_mlp: float32 [1024], replicated, may hold values from 0.1 to 1.9
Outputs:
- result: bfloat16 [16, 1376, 1024], P('shard', 'ctx')
- d_tokens: float32 [16, 1376, 1024], P('shard', 'ctx')
- d_ln1_gain: float32 [1024], replicated
- d_ln1_bias: float32 [1024], replicated
- d_w_qkv: float32 [1024, 3, 1024], P(('shard', 'ctx'), None, 'tp')
- d_b_qv: float32 [2, 1024], P(None, 'tp')
- d_w_proj: float32 [1024, 1024], P(('shard', 'ctx'), 'tp')
- d_b_proj: float32 [1024], replicated
- d_scale_attn: float32 [1024], replicated
- d_ln2_gain: float32 [1024], replicated
- d_ln2_bias: float32 [1024], replicated
- d_w_up: float32 [1024, 4096], P(('shard', 'ctx'), 'tp')
- d_b_up: float32 [4096], P('tp')
- d_w_down: float32 [1024, 4096], P(('shard', 'ctx'), 'tp')
- d_b_down: float32 [1024], replicated
- d_scale_mlp: float32 [1024], replicated
Inputs may be any that keep to these rules, and one draw needn't show every extreme that they name: `slot_live`: each index of shard owns 2 consecutive slots, the first of which always holds an image; exactly 13 slots hold one. `block_rows`: each slot's row of 4 entries sums to 1370.
All inputs are finite; a program needn't handle non-finite values.
Results may differ from a plain program's by a relative error of at most 0.02.
Values may be sent and summed in bfloat16 or wider, within the bound.
No kernel may reach another device: no remote copies, remote signals or barrier semaphores. Data moves between devices by JAX's collectives and lax.ppermute only.
A program may use at most 128 MiB of HBM per device.

v0:
```python
import jax
import jax.numpy as jnp
from jax import lax
from jax.sharding import PartitionSpec as P

HEAD_DIM = 64
EPSILON = 1e-06
MASKED = -1e30


def layer_stats(values):
    average = jnp.mean(values, axis=-1, keepdims=True)
    centered = values - average
    variance = jnp.mean(centered * centered, axis=-1, keepdims=True)
    inverse = lax.rsqrt(variance + EPSILON)
    return (centered * inverse, inverse)


def norm_back(grad_hat, normal_hat, inverse):
    first_term = jnp.mean(grad_hat, axis=-1, keepdims=True)
    second_term = jnp.mean(grad_hat * normal_hat, axis=-1, keepdims=True)
    return inverse * (grad_hat - first_term - normal_hat * second_term)


def tensor_sum(partial_rows):
    return lax.psum(partial_rows, "tp")


def input_sum(partial_rows):
    return lax.psum(partial_rows, "tp")


def attention_scores(queries, all_keys, key_valid, heads_dev):
    slot_count, block_len = (queries.shape[0], queries.shape[1])
    key_count = all_keys.shape[1]
    split_queries = queries.reshape(slot_count, block_len, heads_dev, HEAD_DIM)
    split_keys = all_keys.reshape(slot_count, key_count, heads_dev, HEAD_DIM)
    scores = jnp.einsum(
        "sqhe,skhe->shqk", split_queries, split_keys, preferred_element_type=jnp.float32
    ) * HEAD_DIM ** (-0.5)
    return jnp.where(key_valid[:, None, None, :], scores, MASKED)


def per_device(
    tokens,
    cotangent,
    slot_live,
    block_rows,
    ln1_gain,
    ln1_bias,
    w_qkv,
    b_qv,
    w_proj,
    b_proj,
    scale_attn,
    ln2_gain,
    ln2_bias,
    w_up,
    b_up,
    w_down,
    b_down,
    scale_mlp,
):
    slot_count, block_len, model_width = tokens.shape
    ctx_count = lax.axis_size("ctx")
    key_count = block_len * ctx_count
    heads_dev = w_qkv.shape[2] // HEAD_DIM
    head_width = heads_dev * HEAD_DIM
    positions = jnp.arange(key_count, dtype=jnp.int32)
    owners = positions // block_len
    within = positions % block_len
    matches = owners[:, None] == jnp.arange(ctx_count, dtype=jnp.int32)[None, :]
    counts_at = jnp.sum(jnp.where(matches[None], block_rows[:, None, :], 0), axis=-1)
    key_valid = (within[None, :] < counts_at) & (slot_live[:, None] > 0)
    row_valid = lax.dynamic_slice_in_dim(key_valid, lax.axis_index("ctx") * block_len, block_len, 1)
    row_mask = row_valid.astype(jnp.float32)[..., None]
    full_qkv, full_proj, full_up, full_down = (
        lax.all_gather(w_qkv, ("shard", "ctx"), axis=0, tiled=True),
        lax.all_gather(w_proj, ("shard", "ctx"), axis=0, tiled=True),
        lax.all_gather(w_up, ("shard", "ctx"), axis=0, tiled=True),
        lax.all_gather(w_down, ("shard", "ctx"), axis=0, tiled=True),
    )
    source = tokens.astype(jnp.float32)
    normal_one, inverse_one = layer_stats(source)
    normed = (normal_one * ln1_gain + ln1_bias).astype(jnp.bfloat16)
    shifts = jnp.stack([b_qv[0], jnp.zeros_like(b_qv[0]), b_qv[1]])
    mixed_qkv = (
        jnp.einsum("sbd,dcf->sbcf", normed, full_qkv, preferred_element_type=jnp.float32) + shifts
    ).astype(jnp.bfloat16)
    queries = mixed_qkv[:, :, 0]
    key_rows = mixed_qkv[:, :, 1]
    value_rows = mixed_qkv[:, :, 2]
    all_keys, all_values = (
        lax.all_gather(key_rows, "ctx", axis=1, tiled=True),
        lax.all_gather(value_rows, "ctx", axis=1, tiled=True),
    )
    scores = attention_scores(queries, all_keys, key_valid, heads_dev)
    top_score = jnp.max(scores, axis=-1, keepdims=True)
    exp_scores = jnp.exp(scores - top_score)
    denominator = jnp.sum(exp_scores, axis=-1, keepdims=True)
    log_total = top_score + jnp.log(denominator)
    soft_weights = (exp_scores / denominator).astype(jnp.bfloat16)
    split_values = all_values.reshape(slot_count, key_count, heads_dev, HEAD_DIM)
    attended = jnp.einsum(
        "shqk,skhe->sqhe", soft_weights, split_values, preferred_element_type=jnp.float32
    )
    attended = attended.reshape(slot_count, block_len, head_width).astype(jnp.bfloat16)
    attn_part = jnp.einsum("sbf,df->sbd", attended, full_proj, preferred_element_type=jnp.float32)
    branch_attn = tensor_sum(attn_part) + b_proj
    middle = source + scale_attn * branch_attn
    normal_two, inverse_two = layer_stats(middle)
    second_here = (normal_two * ln2_gain + ln2_bias).astype(jnp.bfloat16)
    hidden = (
        jnp.einsum("sbd,dh->sbh", second_here, full_up, preferred_element_type=jnp.float32) + b_up
    )
    active = jax.nn.gelu(hidden, approximate=False).astype(jnp.bfloat16)
    mlp_part = jnp.einsum("sbh,dh->sbd", active, full_down, preferred_element_type=jnp.float32)
    branch_mlp = tensor_sum(mlp_part) + b_down
    result_here = (row_mask * (middle + scale_mlp * branch_mlp)).astype(jnp.bfloat16)
    grad_out = row_mask * cotangent.astype(jnp.float32)
    grad_scale_mlp = jnp.sum(grad_out * branch_mlp, axis=(0, 1))
    grad_branch_mlp = (grad_out * scale_mlp).astype(jnp.bfloat16)
    grad_b_down = jnp.sum(grad_branch_mlp.astype(jnp.float32), axis=(0, 1))
    grad_w_down = jnp.einsum(
        "sbd,sbh->dh", grad_branch_mlp, active, preferred_element_type=jnp.float32
    )
    grad_active = jnp.einsum(
        "sbd,dh->sbh", grad_branch_mlp, full_down, preferred_element_type=jnp.float32
    )
    gelu_back = jax.vjp(lambda inside: jax.nn.gelu(inside, approximate=False), hidden)[1]
    grad_hidden = gelu_back(grad_active)[0].astype(jnp.bfloat16)
    grad_b_up = jnp.sum(grad_hidden.astype(jnp.float32), axis=(0, 1))
    grad_w_up = jnp.einsum(
        "sbd,sbh->dh", second_here, grad_hidden, preferred_element_type=jnp.float32
    )
    second_part = jnp.einsum(
        "sbh,dh->sbd", grad_hidden, full_up, preferred_element_type=jnp.float32
    )
    grad_second = input_sum(second_part)
    grad_ln2_gain = jnp.sum(grad_second * normal_two, axis=(0, 1))
    grad_ln2_bias = jnp.sum(grad_second, axis=(0, 1))
    grad_middle = grad_out + norm_back(grad_second * ln2_gain, normal_two, inverse_two)
    grad_scale_attn = jnp.sum(grad_middle * branch_attn, axis=(0, 1))
    grad_branch_here = (grad_middle * scale_attn).astype(jnp.bfloat16)
    grad_b_proj = jnp.sum(grad_branch_here.astype(jnp.float32), axis=(0, 1))
    grad_w_proj = jnp.einsum(
        "sbd,sbf->df", grad_branch_here, attended, preferred_element_type=jnp.float32
    )
    grad_attended = jnp.einsum(
        "sbd,df->sbf", grad_branch_here, full_proj, preferred_element_type=jnp.float32
    ).astype(jnp.bfloat16)
    split_grad = grad_attended.reshape(slot_count, block_len, heads_dev, HEAD_DIM)
    scores_again = attention_scores(queries, all_keys, key_valid, heads_dev)
    probs = jnp.exp(scores_again - log_total)
    split_keys = all_keys.reshape(slot_count, key_count, heads_dev, HEAD_DIM)
    split_queries = queries.reshape(slot_count, block_len, heads_dev, HEAD_DIM)
    grad_probs = jnp.einsum(
        "sqhe,skhe->shqk", split_grad, split_values, preferred_element_type=jnp.float32
    )
    row_dot = jnp.sum(probs * grad_probs, axis=-1, keepdims=True)
    grad_scores = (probs * (grad_probs - row_dot)).astype(jnp.bfloat16)
    grad_queries = jnp.einsum(
        "shqk,skhe->sqhe", grad_scores, split_keys, preferred_element_type=jnp.float32
    ) * HEAD_DIM ** (-0.5)
    grad_queries = grad_queries.reshape(slot_count, block_len, head_width).astype(jnp.bfloat16)
    probs_low = probs.astype(jnp.bfloat16)
    grad_values_part = jnp.einsum(
        "shqk,sqhe->skhe", probs_low, split_grad, preferred_element_type=jnp.float32
    )
    grad_keys_part = jnp.einsum(
        "shqk,sqhe->skhe", grad_scores, split_queries, preferred_element_type=jnp.float32
    ) * HEAD_DIM ** (-0.5)
    grad_keys, grad_values = (
        lax.psum_scatter(
            grad_keys_part.reshape(slot_count, key_count, head_width),
            "ctx",
            scatter_dimension=1,
            tiled=True,
        ),
        lax.psum_scatter(
            grad_values_part.reshape(slot_count, key_count, head_width),
            "ctx",
            scatter_dimension=1,
            tiled=True,
        ),
    )
    grad_keys = grad_keys.astype(jnp.bfloat16)
    grad_values = grad_values.astype(jnp.bfloat16)
    grad_mixed = jnp.stack([grad_queries, grad_keys, grad_values], axis=2)
    grad_b_qv = jnp.stack(
        [
            jnp.sum(grad_queries.astype(jnp.float32), axis=(0, 1)),
            jnp.sum(grad_values.astype(jnp.float32), axis=(0, 1)),
        ]
    )
    grad_w_qkv = jnp.einsum("sbd,sbcf->dcf", normed, grad_mixed, preferred_element_type=jnp.float32)
    normed_part = jnp.einsum(
        "sbcf,dcf->sbd", grad_mixed, full_qkv, preferred_element_type=jnp.float32
    )
    grad_normed = input_sum(normed_part)
    grad_ln1_gain = jnp.sum(grad_normed * normal_one, axis=(0, 1))
    grad_ln1_bias = jnp.sum(grad_normed, axis=(0, 1))
    tokens_here = grad_middle + norm_back(grad_normed * ln1_gain, normal_one, inverse_one)
    weight_parts = (
        lax.psum_scatter(grad_w_qkv, ("shard", "ctx"), scatter_dimension=0, tiled=True),
        lax.psum_scatter(grad_w_proj, ("shard", "ctx"), scatter_dimension=0, tiled=True),
        lax.psum_scatter(grad_w_up, ("shard", "ctx"), scatter_dimension=0, tiled=True),
        lax.psum_scatter(grad_w_down, ("shard", "ctx"), scatter_dimension=0, tiled=True),
    )
    small_parts = (
        lax.psum(grad_ln1_gain.astype(jnp.bfloat16), ("shard", "ctx")).astype(jnp.float32),
        lax.psum(grad_ln1_bias.astype(jnp.bfloat16), ("shard", "ctx")).astype(jnp.float32),
        lax.psum(grad_b_qv.astype(jnp.bfloat16), ("shard", "ctx")).astype(jnp.float32),
        lax.psum(grad_b_proj.astype(jnp.bfloat16), ("shard", "ctx")).astype(jnp.float32),
        lax.psum(grad_scale_attn.astype(jnp.bfloat16), ("shard", "ctx")).astype(jnp.float32),
        lax.psum(grad_ln2_gain.astype(jnp.bfloat16), ("shard", "ctx")).astype(jnp.float32),
        lax.psum(grad_ln2_bias.astype(jnp.bfloat16), ("shard", "ctx")).astype(jnp.float32),
        lax.psum(grad_b_up.astype(jnp.bfloat16), ("shard", "ctx")).astype(jnp.float32),
        lax.psum(grad_b_down.astype(jnp.bfloat16), ("shard", "ctx")).astype(jnp.float32),
        lax.psum(grad_scale_mlp.astype(jnp.bfloat16), ("shard", "ctx")).astype(jnp.float32),
    )
    return (
        result_here,
        tokens_here,
        small_parts[0],
        small_parts[1],
        weight_parts[0],
        small_parts[2],
        weight_parts[1],
        small_parts[3],
        small_parts[4],
        small_parts[5],
        small_parts[6],
        weight_parts[2],
        small_parts[7],
        weight_parts[3],
        small_parts[8],
        small_parts[9],
    )


def solution(mesh):
    placed = (
        P("shard", "ctx", None),
        P("shard", "ctx", None),
        P("shard"),
        P("shard", None),
        P(),
        P(),
        P(("shard", "ctx"), None, "tp"),
        P(None, "tp"),
        P(("shard", "ctx"), "tp"),
        P(),
        P(),
        P(),
        P(),
        P(("shard", "ctx"), "tp"),
        P("tp"),
        P(("shard", "ctx"), "tp"),
        P(),
        P(),
    )
    return jax.shard_map(
        per_device,
        mesh=mesh,
        in_specs=placed,
        out_specs=(
            P("shard", "ctx", None),
            P("shard", "ctx", None),
            P(),
            P(),
            P(("shard", "ctx"), None, "tp"),
            P(None, "tp"),
            P(("shard", "ctx"), "tp"),
            P(),
            P(),
            P(),
            P(),
            P(("shard", "ctx"), "tp"),
            P("tp"),
            P(("shard", "ctx"), "tp"),
            P(),
            P(),
        ),
        check_vma=False,
    )
```

profile of v0, /device:TPU:0, one launch (start us, length us, event | category | flops | bytes accessed | tf_op | source)
XLA Modules:
  0.0 1637.6 jit_solution(12294867799143030191)
XLA Ops:
  11.7 153.0 %all-gather.8.cloned.1.call-done = bf16[1024,3,256]{2,0,1:T(8,128)(2,1)} async-done(((bf16[32,3,256]{2,0,1:T(8,128)(2,1)}), bf16[1024,3,256]{2,0,1:T(8,128)(2,1)}) %all-gather.8.cloned.1.call-update) | async-done | bytes 1572880 | tf_op jit(solution)/shard_map/all_gather | solution.py:78
  168.9 83.9 %all_gather.21 = bf16[1024,256]{1,0:T(8,128)(2,1)S(1)} all-gather(bf16[32,256]{1,0:T(8,128)(2,1)S(1)} %copy-done.44), channel_id=1, replica_groups=mesh['shard'=8,'ctx'=4,'tp'=4] {'shard','ctx'}, dimensions={0}, use_global_device_ids=true | all-gather | bytes 540672 | tf_op jit(solution)/shard_map/all_gather | solution.py:79
  255.1 7.9 fusion.64
  263.0 7.8 fusion
  276.0 7.5 fusion.43
  287.6 69.5 %all-reduce.6.cloned.1.call-done = f32[2,344,1024]{2,1,0:T(8,128)} async-done(((f32[2,344,1024]{2,1,0:T(8,128)}), f32[2,344,1024]{2,1,0:T(8,128)}) %all-reduce.6.cloned.1.call-update) | async-done | bytes 2818064 | tf_op jit(solution)/shard_map/psum | solution.py:26
  360.4 151.1 %all-gather.10.cloned.1.call-done = bf16[1024,1024]{1,0:T(8,128)(2,1)} async-done(((bf16[32,1024]{1,0:T(8,128)(2,1)}), bf16[1024,1024]{1,0:T(8,128)(2,1)}) %all-gather.10.cloned.1.call-update) | async-done | bytes 2097168 | tf_op jit(solution)/shard_map/all_gather | solution.py:80
  511.4 4.3 fusion.46
  517.3 7.5 multiply_convert_fusion.4
  524.8 141.5 %all-gather.12.cloned.1.call-done = bf16[1024,1024]{1,0:T(8,128)(2,1)} async-done(((bf16[32,1024]{1,0:T(8,128)(2,1)}), bf16[1024,1024]{1,0:T(8,128)(2,1)}) %all-gather.12.cloned.1.call-update) | async-done | bytes 2097168 | tf_op jit(solution)/shard_map/all_gather | solution.py:81
  666.3 7.1 fusion.66
  678.0 70.6 %all-reduce.8.cloned.1.call-done = f32[2,344,1024]{2,1,0:T(8,128)} async-done(((f32[2,344,1024]{2,1,0:T(8,128)}), f32[2,344,1024]{2,1,0:T(8,128)}) %all-reduce.8.cloned.1.call-update) | async-done | bytes 2818064 | tf_op jit(solution)/shard_map/psum | solution.py:30
  748.6 3.9 multiply_reduce_fusion.2
  752.5 3.5 multiply_reduce_fusion.3
  761.2 8.5 fusion.2
  773.4 7.5 multiply_reduce_fusion
  780.8 7.3 multiply_convert_fusion
  788.2 3.9 convolution_multiply_fusion
  792.2 3.6 copy.63
  796.1 5.4 fusion.28
  801.6 3.7 fusion.65
  808.2 36.8 %reduce-scatter.7.cloned.1.call-done = f32[2,344,256]{2,1,0:T(8,128)} async-done(((f32[2,1376,256]{2,1,0:T(8,128)}), f32[2,344,256]{2,1,0:T(8,128)}) %reduce-scatter.7.cloned.1.call-update) | async-done | bytes 704528 | tf_op jit(solution)/shard_map/reduce_scatter | solution.py:174
  854.0 5.8 convolution_bitcast_fusion.1
  860.5 5.7 convolution_bitcast_fusion
  867.3 4.8 convolution_bitcast_fusion.2
  875.5 90.8 %all-reduce.10.cloned.1.call-done = (f32[2,344,1024]{2,1,0:T(8,128)}, f32[2,344,1024]{2,1,0:T(8,128)}) async-done(((f32[2,344,1024]{2,1,0:T(8,128)}, f32[2,344,1024]{2,1,0:T(8,128)}), (f32[2,344,1024]{2,1,0:T(8,128)}, f32[2,344,1024]{2,1,0:T(8,128)})) %all-reduce.10.cloned.1.call-update) | async-done | bytes 5636112 | tf_op jit(solution)/shard_map/psum | solution.py:26
  966.2 3.8 fusion.18
  972.1 157.4 %all-reduce.1 = (bf16[1024]{0:T(1024)(128)(2,1)S(1)}, bf16[1024]{0:T(1024)(128)(2,1)S(1)}, bf16[2,256]{1,0:T(2,128)(2,1)S(1)}, bf16[1024]{0:T(1024)(128)(2,1)S(1...) all-reduce(bf16[1024]{0:T(1024)(128)(2,1)S(1)} %get-tuple-element.1, ...), channel_id=1, replica_groups=mesh['shard'=8,'ctx'=4,'tp'=4] {'shard','ctx'}, use_global_device_ids=true, to_apply=%region_19.20 | all-reduce | flops 9728 | bytes 38912 | tf_op jit(solution)/shard_map/psum | solution.py:211
  1135.4 4.7 fusion.17
  1140.2 157.8 %reduce-scatter.15.cloned.1.call-done = f32[32,1024]{1,0:T(8,128)} async-done(((f32[1024,1024]{1,0:T(8,128)}), f32[32,1024]{1,0:T(8,128)}) %reduce-scatter.15.cloned.1.call-update) | async-done | bytes 131088 | tf_op jit(solution)/shard_map/reduce_scatter | solution.py:207
  1298.0 167.6 %reduce-scatter.17.cloned.1.call-done = f32[32,1024]{1,0:T(8,128)} async-done(((f32[1024,1024]{1,0:T(8,128)}), f32[32,1024]{1,0:T(8,128)}) %reduce-scatter.17.cloned.1.call-update) | async-done | bytes 131088 | tf_op jit(solution)/shard_map/reduce_scatter | solution.py:208
  1465.6 165.3 %reduce-scatter.11.cloned.1.call-done = f32[32,3,256]{2,0,1:T(8,128)} async-done(((f32[1024,3,256]{2,0,1:T(8,128)}), f32[32,3,256]{2,0,1:T(8,128)}) %reduce-scatter.11.cloned.1.call-update) | async-done | bytes 98320 | tf_op jit(solution)/shard_map/reduce_scatter | solution.py:205
  (217 shorter events, 63.7 us)
Async XLA Ops:
  7.2 157.5 %copy-start.3 = (bf16[2,344,1024]{2,1,0:T(8,128)(2,1)S(1)}, bf16[2,344,1024]{2,1,0:T(8,128)(2,1)}, u32[]{:S(2)}) copy-start(bf16[2,344,1024]{2,1,0:T(8,128)(2,1)} %param.18) | copy-start | bytes 4227076
  7.2 157.5 %copy-start.38 = (f32[1024]{0:T(1024)S(1)}, f32[1024]{0:T(1024)}, u32[]{:S(2)}) copy-start(f32[1024]{0:T(1024)} %param.22) | copy-start | bytes 12292
  7.2 157.5 %copy-start.59 = (f32[1024]{0:T(1024)S(1)}, f32[1024]{0:T(1024)}, u32[]{:S(2)}) copy-start(f32[1024]{0:T(1024)} %param.23) | copy-start | bytes 12292
  7.2 157.5 %all-gather.8.cloned.1.call-start = ((), (), s32[]{:S(2)}) async-start(), calls=%async_computation.6 | async-start | bytes 1622016 | tf_op jit(solution)/shard_map/all_gather | solution.py:78
  8.0 245.3 %all-gather.16.cloned.1.call-start = ((), (), s32[]{:S(2)}) async-start(), calls=%async_computation.18 | async-start | bytes 1761280 | tf_op jit(solution)/shard_map/all_gather | solution.py:94
  9.7 158.0 %copy-start.28 = (f32[2,344]{1,0:T(2,128)}, f32[2,344]{1,0:T(2,128)S(1)}, u32[]{:S(2)}) copy-start(f32[2,344]{1,0:T(2,128)S(1)} %broadcast_multiply_fusion.5) | copy-start | bytes 8260
  11.7 156.1 %copy-start.32 = (f32[2,344]{1,0:T(2,128)}, f32[2,344]{1,0:T(2,128)S(1)}, u32[]{:S(2)}) copy-start(f32[2,344]{1,0:T(2,128)S(1)} %add_rsqrt_fusion.1) | copy-start | bytes 8260
  11.7 157.1 %copy-start.54 = (s32[2,4]{1,0:T(2,128)S(1)}, s32[2,4]{1,0:T(2,128)}, u32[]{:S(2)}) copy-start(s32[2,4]{1,0:T(2,128)} %param.21) | copy-start | bytes 100
  11.7 157.2 %copy-start.44 = (bf16[32,256]{1,0:T(8,128)(2,1)S(1)}, bf16[32,256]{1,0:T(8,128)(2,1)}, u32[]{:S(2)}) copy-start(bf16[32,256]{1,0:T(8,128)(2,1)} %param.26) | copy-start | bytes 49156
  167.8 85.2 %copy-start.61 = (s32[2]{0:T(128)S(1)}, s32[2]{0:T(128)}, u32[]{:S(2)}) copy-start(s32[2]{0:T(128)} %param.20) | copy-start | bytes 28
  168.7 105.5 %all-gather.14.cloned.1.call-start = ((), (), s32[]{:S(2)}) async-start(), calls=%async_computation.17 | async-start | bytes 1761280 | tf_op jit(solution)/shard_map/all_gather | solution.py:95
  252.8 104.3 %all-reduce.6.cloned.1.call-start = ((), (), s32[]{:S(2)}) async-start(), calls=%async_computation.7 | async-start | bytes 5636096 | tf_op jit(solution)/shard_map/psum | solution.py:26
  283.5 73.6 %copy-start.36 = (f32[1024]{0:T(1024)S(1)}, f32[1024]{0:T(1024)}, u32[]{:S(2)}) copy-start(f32[1024]{0:T(1024)} %param.27) | copy-start | bytes 12292
  285.8 225.6 %all-gather.10.cloned.1.call-start = ((), (), s32[]{:S(2)}) async-start(), calls=%async_computation.8 | async-start | bytes 2162688 | tf_op jit(solution)/shard_map/all_gather | solution.py:80
  286.4 379.9 %all-gather.12.cloned.1.call-start = ((), (), s32[]{:S(2)}) async-start(), calls=%async_computation.9 | async-start | bytes 2162688 | tf_op jit(solution)/shard_map/all_gather | solution.py:81
  287.0 461.7 %all-reduce.8.cloned.1.call-start = ((), (), s32[]{:S(2)}) async-start(), calls=%async_computation.10 | async-start | bytes 5636096 | tf_op jit(solution)/shard_map/psum | solution.py:30
  287.6 464.9 %copy-start.26 = (f32[2,344]{1,0:T(2,128)}, f32[2,344]{1,0:T(2,128)S(1)}, u32[]{:S(2)}) copy-start(f32[2,344]{1,0:T(2,128)S(1)} %dynamic-slice_convert_fusion) | copy-start | bytes 8260
  359.9 392.6 %copy-start.1 = (f32[2,344,1024]{2,1,0:T(8,128)}, f32[2,344,1024]{2,1,0:T(8,128)S(1)}, u32[]{:S(2)}) copy-start(f32[2,344,1024]{2,1,0:T(8,128)S(1)} %get-tuple-element.45) | copy-start | bytes 8454148
  359.9 151.6 %copy-start.40 = (f32[1024]{0:T(1024)S(1)}, f32[1024]{0:T(1024)}, u32[]{:S(2)}) copy-start(f32[1024]{0:T(1024)} %param.29) | copy-start | bytes 12292
  359.9 151.6 %copy-start.49 = (f32[1024]{0:T(1024)S(1)}, f32[1024]{0:T(1024)}, u32[]{:S(2)}) copy-start(f32[1024]{0:T(1024)} %param.32) | copy-start | bytes 12292
  359.9 151.6 %copy-start.57 = (f32[1024]{0:T(1024)S(1)}, f32[1024]{0:T(1024)}, u32[]{:S(2)}) copy-start(f32[1024]{0:T(1024)} %param.30) | copy-start | bytes 12292
  359.9 392.6 %copy-start.30 = (f32[2,344]{1,0:T(2,128)}, f32[2,344]{1,0:T(2,128)S(1)}, u32[]{:S(2)}) copy-start(f32[2,344]{1,0:T(2,128)S(1)} %broadcast_multiply_fusion.4) | copy-start | bytes 8260
  360.4 392.2 %copy-start.34 = (f32[2,344]{1,0:T(2,128)}, f32[2,344]{1,0:T(2,128)S(1)}, u32[]{:S(2)}) copy-start(f32[2,344]{1,0:T(2,128)S(1)} %add_rsqrt_fusion) | copy-start | bytes 8260
  517.3 149.0 %copy-start.42 = (f32[1024]{0:T(1024)S(1)}, f32[1024]{0:T(1024)}, u32[]{:S(2)}) copy-start(f32[1024]{0:T(1024)} %param.35) | copy-start | bytes 12292
  677.8 129.3 %reduce-scatter.9.cloned.1.call-start = ((), (), s32[]{:S(2)}) async-start(), calls=%async_computation.12 | async-start | bytes 3522560 | tf_op jit(solution)/shard_map/reduce_scatter | solution.py:180
  772.0 73.0 %reduce-scatter.7.cloned.1.call-start = ((), (), s32[]{:S(2)}) async-start(), calls=%async_computation.11 | async-start | bytes 3522560 | tf_op jit(solution)/shard_map/reduce_scatter | solution.py:174
  795.8 170.4 %all-reduce.10.cloned.1.call-start = ((), (), s32[]{:S(2)}) async-start(), calls=%async_computation.19 | async-start | bytes 11272192 | tf_op jit(solution)/shard_map/psum | solution.py:26
  849.9 290.3 %reduce-scatter.13.cloned.1.call-start = ((), (), s32[]{:S(2)}) async-start(), calls=%async_computation.14 | async-start | bytes 1081344 | tf_op jit(solution)/shard_map/reduce_scatter | solution.py:206
  853.9 444.1 %reduce-scatter.15.cloned.1.call-start = ((), (), s32[]{:S(2)}) async-start(), calls=%async_computation.15 | async-start | bytes 4325376 | tf_op jit(solution)/shard_map/reduce_scatter | solution.py:207
  859.8 605.8 %reduce-scatter.17.cloned.1.call-start = ((), (), s32[]{:S(2)}) async-start(), calls=%async_computation.16 | async-start | bytes 4325376 | tf_op jit(solution)/shard_map/reduce_scatter | solution.py:208
  866.2 764.6 %reduce-scatter.11.cloned.1.call-start = ((), (), s32[]{:S(2)}) async-start(), calls=%async_computation.13 | async-start | bytes 3244032 | tf_op jit(solution)/shard_map/reduce_scatter | solution.py:205
  874.0 96.0 %copy-start.50 = (f32[1024]{0:T(1024)S(1)}, f32[1024]{0:T(1024)}, u32[]{:S(2)}) copy-start(f32[1024]{0:T(1024)} %param.34) | copy-start | bytes 12292
  (47 other events, 357.5 us)
Sparse Core Ops, SparseCore 0:
  9.7 154.9 all-gather.7
  168.8 26.0 all-gather.15
  253.0 21.1 all-gather.13
  285.9 71.1 all-reduce.5
  358.7 152.6 all-gather.9
  513.0 153.2 all-gather.11
  677.9 70.6 all-reduce.7
  772.1 34.9 reduce-scatter.8
  809.7 35.2 reduce-scatter.6
  850.0 116.2 all-reduce.9
  969.2 160.6 reduce-scatter.12
  1132.8 165.1 reduce-scatter.14
  1301.1 164.4 reduce-scatter.16
  1468.5 162.2 reduce-scatter.10
where the time goes:
time: 1650 us; the launch traced here: 1640 us
  waiting for transfers between devices  1210 us (73%)
  blocking collectives  241 us (15%)
  matrix products  86.9 us (5%)
  other arithmetic  59.4 us (4%)
  local copies, waits for them, and re-layouts  23.7 us (1%)
    reduce_scatter x1, waiting for transfers between devices, per_device(): lax.psum_scatter(grad_w_down, ('shard', 'ctx'), scatter_dimension=0, tile...  168 us
    reduce_scatter x1, waiting for transfers between devices, per_device(): lax.psum_scatter(grad_w_qkv, ('shard', 'ctx'), scatter_dimension=0, tiled...  165 us
    psum x2, waiting for transfers between devices, tensor_sum(): return lax.psum(partial_rows, 'tp')  160 us
    reduce_scatter x1, waiting for transfers between devices, per_device(): lax.psum_scatter(grad_w_up, ('shard', 'ctx'), scatter_dimension=0, tiled=...  158 us
    psum x1, blocking collectives, per_device(): lax.psum(grad_ln1_gain.astype(jnp.bfloat16), ('shard', 'ctx'))  157 us
    all_gather x1, waiting for transfers between devices, per_device(): lax.all_gather(w_qkv, ('shard', 'ctx'), axis=0, tiled=True)  153 us
    all_gather x1, waiting for transfers between devices, per_device(): lax.all_gather(w_up, ('shard', 'ctx'), axis=0, tiled=True)  151 us
    all_gather x1, waiting for transfers between devices, per_device(): lax.all_gather(w_down, ('shard', 'ctx'), axis=0, tiled=True)  141 us
  transfers between devices with their start and end apart: 14, of which 12 were waited for; matrix products, arithmetic and copies ran while one was open for 7% of the time, Pallas kernels for 0%

commit v1 on v0

--- a/solution.py
+++ b/solution.py
@@ -76,7 +76,12 @@
     row_mask = row_valid.astype(jnp.float32)[..., None]
     full_qkv, full_proj, full_up, full_down = (
         lax.all_gather(w_qkv, ("shard", "ctx"), axis=0, tiled=True),
-        lax.all_gather(w_proj, ("shard", "ctx"), axis=0, tiled=True),
+        jnp.concatenate(
+            lax.all_to_all(
+                jnp.stack([w_proj] * lax.axis_size(("shard", "ctx"))), ("shard", "ctx"), 0, 0
+            ),
+            axis=0,
+        ),
         lax.all_gather(w_up, ("shard", "ctx"), axis=0, tiled=True),
         lax.all_gather(w_down, ("shard", "ctx"), axis=0, tiled=True),
     )

time: 1650 us -> 1600 us (0.970)
  blocking collectives: 241 us -> 157 us
  waiting for transfers between devices: 1210 us -> 1230 us
    all_gather x1 -> x0, blocking collectives: 83.9 us -> none  [per_device(): lax.all_gather(w_proj, ('shard', 'ctx'), axis=0, tiled=True)]
    all_gather x1, waiting for transfers between devices: 0.02 us -> 18.1 us  [per_device(): lax.all_gather(key_rows, 'ctx', axis=1, tiled=True)]
  transfers between devices with their start and end apart: 14 -> 15, of which waited for: 12 -> 13; matrix products, arithmetic and copies ran while one was open for 7% -> 8% of each run, Pallas kernels for 0% -> 0%
where the time goes in v1:
time: 1600 us; the launch traced here: 1590 us
  waiting for transfers between devices  1230 us (77%)
  blocking collectives  157 us (10%)
  matrix products  86.9 us (5%)
  other arithmetic  59.6 us (4%)
  local copies, waits for them, and re-layouts  24.5 us (2%)
    reduce_scatter x1, waiting for transfers between devices, per_device(): lax.psum_scatter(grad_w_down, ('shard', 'ctx'), scatter_dimension=0, tile...  168 us
    reduce_scatter x1, waiting for transfers between devices, per_device(): lax.psum_scatter(grad_w_qkv, ('shard', 'ctx'), scatter_dimension=0, tiled...  165 us
    psum x2, waiting for transfers between devices, tensor_sum(): return lax.psum(partial_rows, 'tp')  160 us
    reduce_scatter x1, waiting for transfers between devices, per_device(): lax.psum_scatter(grad_w_up, ('shard', 'ctx'), scatter_dimension=0, tiled=...  158 us
    psum x1, blocking collectives, per_device(): lax.psum(grad_ln1_gain.astype(jnp.bfloat16), ('shard', 'ctx'))  157 us
    all_gather x1, waiting for transfers between devices, per_device(): lax.all_gather(w_qkv, ('shard', 'ctx'), axis=0, tiled=True)  153 us
    all_gather x1, waiting for transfers between devices, per_device(): lax.all_gather(w_up, ('shard', 'ctx'), axis=0, tiled=True)  151 us
    all_gather x1, waiting for transfers between devices, per_device(): lax.all_gather(w_down, ('shard', 'ctx'), axis=0, tiled=True)  142 us
  transfers between devices with their start and end apart: 15, of which 13 were waited for; matrix products, arithmetic and copies ran while one was open for 8% of the time, Pallas kernels for 0%

profile of v1, /device:TPU:0, one launch (start us, length us, event | category | flops | bytes accessed | tf_op | source)
XLA Modules:
  0.0 1586.4 jit_solution(15693755594445421938)
XLA Ops:
  11.7 153.4 %all-gather.8.cloned.1.call-done = bf16[1024,3,256]{2,0,1:T(8,128)(2,1)} async-done(((bf16[32,3,256]{2,0,1:T(8,128)(2,1)}), bf16[1024,3,256]{2,0,1:T(8,128)(2,1)}) %all-gather.8.cloned.1.call-update) | async-done | bytes 1572880 | tf_op jit(solution)/shard_map/all_gather | solution.py:78
  170.0 6.7 all-to-all-start
  177.8 18.1 %all-gather.16.cloned.1.call-done = bf16[2,1376,1,256]{3,1,2,0:T(8,128)(2,1)} async-done(((bf16[2,344,1,256]{3,1,2,0:T(8,128)(2,1)}), bf16[2,1376,1,256]{3,1,2,0:T(8,128)(2,1)}) %all-gather.16.cloned.1.call-update) | async-done | bytes 1409040 | tf_op jit(solution)/shard_map/all_gather | solution.py:99
  197.7 7.9 fusion.61
  205.6 8.0 fusion
  213.6 9.2 all-gather.14.cloned.1.call-done
  224.6 7.5 fusion.43
  236.2 69.5 %all-reduce.6.cloned.1.call-done = f32[2,344,1024]{2,1,0:T(8,128)} async-done(((f32[2,344,1024]{2,1,0:T(8,128)}), f32[2,344,1024]{2,1,0:T(8,128)}) %all-reduce.6.cloned.1.call-update) | async-done | bytes 2818064 | tf_op jit(solution)/shard_map/psum | solution.py:26
  309.0 151.1 %all-gather.10.cloned.1.call-done = bf16[1024,1024]{1,0:T(8,128)(2,1)} async-done(((bf16[32,1024]{1,0:T(8,128)(2,1)}), bf16[1024,1024]{1,0:T(8,128)(2,1)}) %all-gather.10.cloned.1.call-update) | async-done | bytes 2097168 | tf_op jit(solution)/shard_map/all_gather | solution.py:85
  460.0 4.3 fusion.46
  465.9 7.5 multiply_convert_fusion.4
  473.4 141.6 %all-gather.12.cloned.1.call-done = bf16[1024,1024]{1,0:T(8,128)(2,1)} async-done(((bf16[32,1024]{1,0:T(8,128)(2,1)}), bf16[1024,1024]{1,0:T(8,128)(2,1)}) %all-gather.12.cloned.1.call-update) | async-done | bytes 2097168 | tf_op jit(solution)/shard_map/all_gather | solution.py:86
  615.0 7.1 fusion.63
  626.7 70.5 %all-reduce.8.cloned.1.call-done = f32[2,344,1024]{2,1,0:T(8,128)} async-done(((f32[2,344,1024]{2,1,0:T(8,128)}), f32[2,344,1024]{2,1,0:T(8,128)}) %all-reduce.8.cloned.1.call-update) | async-done | bytes 2818064 | tf_op jit(solution)/shard_map/psum | solution.py:30
  697.2 3.9 multiply_reduce_fusion.2
  709.8 8.5 fusion.2
  722.0 7.5 multiply_reduce_fusion
  729.4 7.3 multiply_convert_fusion
  736.8 3.9 convolution_multiply_fusion
  744.7 5.4 fusion.28
  750.2 3.7 fusion.62
  756.8 36.7 %reduce-scatter.7.cloned.1.call-done = f32[2,344,256]{2,1,0:T(8,128)} async-done(((f32[2,1376,256]{2,1,0:T(8,128)}), f32[2,344,256]{2,1,0:T(8,128)}) %reduce-scatter.7.cloned.1.call-update) | async-done | bytes 704528 | tf_op jit(solution)/shard_map/reduce_scatter | solution.py:179
  802.5 5.8 convolution_bitcast_fusion.1
  809.0 5.7 convolution_bitcast_fusion
  815.8 4.8 convolution_bitcast_fusion.2
  824.0 90.8 %all-reduce.10.cloned.1.call-done = (f32[2,344,1024]{2,1,0:T(8,128)}, f32[2,344,1024]{2,1,0:T(8,128)}) async-done(((f32[2,344,1024]{2,1,0:T(8,128)}, f32[2,344,1024]{2,1,0:T(8,128)}), (f32[2,344,1024]{2,1,0:T(8,128)}, f32[2,344,1024]{2,1,0:T(8,128)})) %all-reduce.10.cloned.1.call-update) | async-done | bytes 5636112 | tf_op jit(solution)/shard_map/psum | solution.py:26
  914.8 3.8 fusion.18
  920.7 157.4 %all-reduce.1 = (bf16[1024]{0:T(1024)(128)(2,1)S(1)}, bf16[1024]{0:T(1024)(128)(2,1)S(1)}, bf16[2,256]{1,0:T(2,128)(2,1)S(1)}, bf16[1024]{0:T(1024)(128)(2,1)S(1...) all-reduce(bf16[1024]{0:T(1024)(128)(2,1)S(1)} %get-tuple-element.1, ...), channel_id=1, replica_groups=mesh['shard'=8,'ctx'=4,'tp'=4] {'shard','ctx'}, use_global_device_ids=true, to_apply=%region_19.20 | all-reduce | flops 9728 | bytes 38912 | tf_op jit(solution)/shard_map/psum | solution.py:216
  1084.0 4.7 fusion.17
  1088.7 157.8 %reduce-scatter.15.cloned.1.call-done = f32[32,1024]{1,0:T(8,128)} async-done(((f32[1024,1024]{1,0:T(8,128)}), f32[32,1024]{1,0:T(8,128)}) %reduce-scatter.15.cloned.1.call-update) | async-done | bytes 131088 | tf_op jit(solution)/shard_map/reduce_scatter | solution.py:212
  1246.6 167.6 %reduce-scatter.17.cloned.1.call-done = f32[32,1024]{1,0:T(8,128)} async-done(((f32[1024,1024]{1,0:T(8,128)}), f32[32,1024]{1,0:T(8,128)}) %reduce-scatter.17.cloned.1.call-update) | async-done | bytes 131088 | tf_op jit(solution)/shard_map/reduce_scatter | solution.py:213
  1414.1 165.3 %reduce-scatter.11.cloned.1.call-done = f32[32,3,256]{2,0,1:T(8,128)} async-done(((f32[1024,3,256]{2,0,1:T(8,128)}), f32[32,3,256]{2,0,1:T(8,128)}) %reduce-scatter.11.cloned.1.call-update) | async-done | bytes 98320 | tf_op jit(solution)/shard_map/reduce_scatter | solution.py:210
  (219 shorter events, 68.6 us)
Async XLA Ops:
  7.2 157.9 %copy-start.3 = (bf16[2,344,1024]{2,1,0:T(8,128)(2,1)S(1)}, bf16[2,344,1024]{2,1,0:T(8,128)(2,1)}, u32[]{:S(2)}) copy-start(bf16[2,344,1024]{2,1,0:T(8,128)(2,1)} %param.18) | copy-start | bytes 4227076
  7.2 157.9 %copy-start.38 = (f32[1024]{0:T(1024)S(1)}, f32[1024]{0:T(1024)}, u32[]{:S(2)}) copy-start(f32[1024]{0:T(1024)} %param.22) | copy-start | bytes 12292
  7.2 157.9 %copy-start.59 = (f32[1024]{0:T(1024)S(1)}, f32[1024]{0:T(1024)}, u32[]{:S(2)}) copy-start(f32[1024]{0:T(1024)} %param.23) | copy-start | bytes 12292
  7.2 157.9 %all-gather.8.cloned.1.call-start = ((), (), s32[]{:S(2)}) async-start(), calls=%async_computation.7 | async-start | bytes 1622016 | tf_op jit(solution)/shard_map/all_gather | solution.py:78
  8.0 187.9 %all-gather.16.cloned.1.call-start = ((), (), s32[]{:S(2)}) async-start(), calls=%async_computation.19 | async-start | bytes 1761280 | tf_op jit(solution)/shard_map/all_gather | solution.py:99
  9.7 158.4 %copy-start.28 = (f32[2,344]{1,0:T(2,128)}, f32[2,344]{1,0:T(2,128)S(1)}, u32[]{:S(2)}) copy-start(f32[2,344]{1,0:T(2,128)S(1)} %broadcast_multiply_fusion.5) | copy-start | bytes 8260
  11.7 156.5 %copy-start.32 = (f32[2,344]{1,0:T(2,128)}, f32[2,344]{1,0:T(2,128)S(1)}, u32[]{:S(2)}) copy-start(f32[2,344]{1,0:T(2,128)S(1)} %add_rsqrt_fusion.1) | copy-start | bytes 8260
  11.7 157.5 %copy-start.44 = (bf16[32,256]{1,0:T(8,128)(2,1)S(1)}, bf16[32,256]{1,0:T(8,128)(2,1)}, u32[]{:S(2)}) copy-start(bf16[32,256]{1,0:T(8,128)(2,1)} %param.26) | copy-start | bytes 49156
  170.0 62.1 %all-to-all-start = ((bf16[32,32,256]{2,1,0:T(8,128)(2,1)}), bf16[32,32,256]{2,1,0:T(8,128)(2,1)S(1)}, u32[]{:S(2)}, u32[]{:S(2)}) async-start(bf16[32,32,256]{2,1,0:T(8,128)(2,1)} %stack.20), calls=%async_computation | async-start | bytes 1048576 | tf_op jit(solution)/shard_map/all_to_all | solution.py:80
  176.7 46.1 %all-gather.14.cloned.1.call-start = ((), (), s32[]{:S(2)}) async-start(), calls=%async_computation.18 | async-start | bytes 1761280 | tf_op jit(solution)/shard_map/all_gather | solution.py:100
  177.4 128.3 %all-reduce.6.cloned.1.call-start = ((), (), s32[]{:S(2)}) async-start(), calls=%async_computation.8 | async-start | bytes 5636096 | tf_op jit(solution)/shard_map/psum | solution.py:26
  232.1 73.6 %copy-start.36 = (f32[1024]{0:T(1024)S(1)}, f32[1024]{0:T(1024)}, u32[]{:S(2)}) copy-start(f32[1024]{0:T(1024)} %param.27) | copy-start | bytes 12292
  232.1 73.6 %copy-start.37 = (f32[1024]{0:T(1024)S(1)}, f32[1024]{0:T(1024)}, u32[]{:S(2)}) copy-start(f32[1024]{0:T(1024)} %param.28) | copy-start | bytes 12292
  234.4 225.6 %all-gather.10.cloned.1.call-start = ((), (), s32[]{:S(2)}) async-start(), calls=%async_computation.9 | async-start | bytes 2162688 | tf_op jit(solution)/shard_map/all_gather | solution.py:85
  235.0 380.0 %all-gather.12.cloned.1.call-start = ((), (), s32[]{:S(2)}) async-start(), calls=%async_computation.10 | async-start | bytes 2162688 | tf_op jit(solution)/shard_map/all_gather | solution.py:86
  235.6 461.6 %all-reduce.8.cloned.1.call-start = ((), (), s32[]{:S(2)}) async-start(), calls=%async_computation.11 | async-start | bytes 5636096 | tf_op jit(solution)/shard_map/psum | solution.py:30
  236.2 464.9 %copy-start.26 = (f32[2,344]{1,0:T(2,128)}, f32[2,344]{1,0:T(2,128)S(1)}, u32[]{:S(2)}) copy-start(f32[2,344]{1,0:T(2,128)S(1)} %dynamic-slice_convert_fusion) | copy-start | bytes 8260
  308.5 392.6 %copy-start.1 = (f32[2,344,1024]{2,1,0:T(8,128)}, f32[2,344,1024]{2,1,0:T(8,128)S(1)}, u32[]{:S(2)}) copy-start(f32[2,344,1024]{2,1,0:T(8,128)S(1)} %get-tuple-element.45) | copy-start | bytes 8454148
  308.5 151.6 %copy-start.40 = (f32[1024]{0:T(1024)S(1)}, f32[1024]{0:T(1024)}, u32[]{:S(2)}) copy-start(f32[1024]{0:T(1024)} %param.29) | copy-start | bytes 12292
  308.5 151.6 %copy-start.49 = (f32[1024]{0:T(1024)S(1)}, f32[1024]{0:T(1024)}, u32[]{:S(2)}) copy-start(f32[1024]{0:T(1024)} %param.32) | copy-start | bytes 12292
  308.5 151.6 %copy-start.57 = (f32[1024]{0:T(1024)S(1)}, f32[1024]{0:T(1024)}, u32[]{:S(2)}) copy-start(f32[1024]{0:T(1024)} %param.30) | copy-start | bytes 12292
  308.5 392.6 %copy-start.30 = (f32[2,344]{1,0:T(2,128)}, f32[2,344]{1,0:T(2,128)S(1)}, u32[]{:S(2)}) copy-start(f32[2,344]{1,0:T(2,128)S(1)} %broadcast_multiply_fusion.4) | copy-start | bytes 8260
  309.0 392.2 %copy-start.34 = (f32[2,344]{1,0:T(2,128)}, f32[2,344]{1,0:T(2,128)S(1)}, u32[]{:S(2)}) copy-start(f32[2,344]{1,0:T(2,128)S(1)} %add_rsqrt_fusion) | copy-start | bytes 8260
  465.9 149.1 %copy-start.42 = (f32[1024]{0:T(1024)S(1)}, f32[1024]{0:T(1024)}, u32[]{:S(2)}) copy-start(f32[1024]{0:T(1024)} %param.35) | copy-start | bytes 12292
  626.5 129.2 %reduce-scatter.9.cloned.1.call-start = ((), (), s32[]{:S(2)}) async-start(), calls=%async_computation.13 | async-start | bytes 3522560 | tf_op jit(solution)/shard_map/reduce_scatter | solution.py:185
  720.6 73.0 %reduce-scatter.7.cloned.1.call-start = ((), (), s32[]{:S(2)}) async-start(), calls=%async_computation.12 | async-start | bytes 3522560 | tf_op jit(solution)/shard_map/reduce_scatter | solution.py:179
  744.4 170.4 %all-reduce.10.cloned.1.call-start = ((), (), s32[]{:S(2)}) async-start(), calls=%async_computation.20 | async-start | bytes 11272192 | tf_op jit(solution)/shard_map/psum | solution.py:26
  798.4 290.3 %reduce-scatter.13.cloned.1.call-start = ((), (), s32[]{:S(2)}) async-start(), calls=%async_computation.15 | async-start | bytes 1081344 | tf_op jit(solution)/shard_map/reduce_scatter | solution.py:211
  802.4 444.1 %reduce-scatter.15.cloned.1.call-start = ((), (), s32[]{:S(2)}) async-start(), calls=%async_computation.16 | async-start | bytes 4325376 | tf_op jit(solution)/shard_map/reduce_scatter | solution.py:212
  808.3 605.8 %reduce-scatter.17.cloned.1.call-start = ((), (), s32[]{:S(2)}) async-start(), calls=%async_computation.17 | async-start | bytes 4325376 | tf_op jit(solution)/shard_map/reduce_scatter | solution.py:213
  814.8 764.6 %reduce-scatter.11.cloned.1.call-start = ((), (), s32[]{:S(2)}) async-start(), calls=%async_computation.14 | async-start | bytes 3244032 | tf_op jit(solution)/shard_map/reduce_scatter | solution.py:210
  822.5 96.0 %copy-start.50 = (f32[1024]{0:T(1024)S(1)}, f32[1024]{0:T(1024)}, u32[]{:S(2)}) copy-start(f32[1024]{0:T(1024)} %param.34) | copy-start | bytes 12292
  (48 other events, 273.2 us)
Sparse Core Ops, SparseCore 0:
  9.7 155.3 all-gather.7
  169.3 26.5 all-gather.15
  197.5 25.2 all-gather.13
  234.5 71.1 all-reduce.5
  307.3 152.6 all-gather.9
  461.6 153.3 all-gather.11
  626.6 70.5 all-reduce.7
  720.7 34.9 reduce-scatter.8
  758.2 35.2 reduce-scatter.6
  798.5 116.2 all-reduce.9
  917.7 160.6 reduce-scatter.12
  1081.4 165.1 reduce-scatter.14
  1249.6 164.4 reduce-scatter.16
  1417.1 162.2 reduce-scatter.10
